TPU v7x, 128 devices: a whole 4x4x4 slice. The times are simulated.
128 devices in a mesh: row: 16 (over y, z), col: 8 (over x, core).
Axes of the slice: x: 4, y: 4, z: 4, core: 2. Of those that a mesh axis runs over, the one named last changes fastest.
Arguments:
- tokens: bfloat16 [2048, 4096], P('row', 'col'), may hold values from -6 to 6
- w_in: bfloat16 [4096, 16384], P('col', 'row'), may hold values from -0.09375 to 0.09375
- w_out: bfloat16 [16384, 4096], P('row', 'col'), may hold values from -0.046875 to 0.046875
- cotangent: bfloat16 [2048, 4096], P('row', 'col'), may hold values from -6 to 6
Outputs:
- block_out: bfloat16 [2048, 4096], P(('row', 'col'))
- grad_tokens: bfloat16 [2048, 4096], P('row', 'col')
- grad_in: float32 [4096, 16384], P('col', 'row')
- grad_out: float32 [16384, 4096], P('row', 'col')
All inputs are finite; a program needn't handle non-finite values.
Results may differ from a plain program's by a relative error of at most 0.015.
Values may be sent and summed in bfloat16 or wider, within the bound.
A program may use at most 128 MiB of HBM per device.

v0:
```python
import jax
import jax.numpy as jnp
from jax import lax
from jax.sharding import PartitionSpec as P


def gelu_grad(value):
    cdf = 0.5 * (1.0 + jax.scipy.special.erf(value * 0.7071067811865476))
    pdf = jnp.exp(-0.5 * value * value) * 0.3989422804014327
    return cdf + value * pdf


def token_panel(local_rows):
    return lax.all_gather(local_rows, "row", axis=0, tiled=True)


def token_panel_a2a(local_rows):
    n = lax.axis_size("row")
    copies = jnp.broadcast_to(local_rows[None], (n,) + local_rows.shape)
    copies = copies.reshape(n * local_rows.shape[0], local_rows.shape[1])
    return lax.all_to_all(copies, "row", split_axis=0, concat_axis=0, tiled=True)


def hidden_panel(local_rows):
    return lax.all_gather(local_rows, "col", axis=0, tiled=True)


def contract_last(left, right):
    return lax.dot_general(
        left, right, (((1,), (1,)), ((), ())), preferred_element_type=jnp.float32
    )


def width_split(left_all, right, transposed):
    if transposed:
        term = contract_last(left_all, right)
    else:
        term = jnp.dot(left_all, right, preferred_element_type=jnp.float32)
    return lax.psum_scatter(
        term.astype(jnp.bfloat16), "col", scatter_dimension=0, tiled=True
    ).astype(jnp.float32)


def unit_sum(left_all, right, transposed):
    n = lax.axis_size("row")
    if transposed:
        term = contract_last(left_all, right)
    else:
        term = jnp.dot(left_all, right, preferred_element_type=jnp.float32)
    pieces = term.astype(jnp.bfloat16).reshape(n, term.shape[0] // n, term.shape[1])
    pieces = lax.all_to_all(pieces, "row", split_axis=0, concat_axis=0, tiled=True)
    return jnp.sum(pieces.astype(jnp.float32), axis=0)


def local(tokens, w_in, w_out, cotangent):
    tokens_all = token_panel(tokens)
    upstream_all = token_panel_a2a(cotangent)
    pre_part = width_split(tokens_all, w_in, False)
    act_all = hidden_panel(jax.nn.gelu(pre_part, approximate=False).astype(jnp.bfloat16))
    dact_part = width_split(upstream_all, w_out, True)
    dpre_all = hidden_panel((dact_part * gelu_grad(pre_part)).astype(jnp.bfloat16))
    mixed = unit_sum(act_all, w_out, False)
    block_rows = (tokens.astype(jnp.float32) + mixed).astype(jnp.bfloat16)
    block_out = lax.all_to_all(block_rows, "col", split_axis=0, concat_axis=1, tiled=True)
    grad_out = lax.dot_general(
        act_all, upstream_all, (((0,), (0,)), ((), ())), preferred_element_type=jnp.float32
    )
    grad_in = lax.dot_general(
        tokens_all, dpre_all, (((0,), (0,)), ((), ())), preferred_element_type=jnp.float32
    )
    back = unit_sum(dpre_all, w_in, True)
    grad_tokens = (cotangent.astype(jnp.float32) + back).astype(jnp.bfloat16)
    return (block_out, grad_tokens, grad_in, grad_out)


def solution(mesh):
    in_specs = (P("row", "col"), P("col", "row"), P("row", "col"), P("row", "col"))
    out_specs = (P(("row", "col"), None), P("row", "col"), P("col", "row"), P("row", "col"))
    return jax.shard_map(local, mesh=mesh, in_specs=in_specs, out_specs=out_specs, check_vma=False)
```

profile of v0, /device:TPU:1, one launch (start us, length us, event | category | flops | bytes accessed | tf_op | source)
XLA Modules:
  0.0 260.2 jit_solution(16874489885100301524)
XLA Ops:
  8.0 0.0 copy-start
  8.0 0.0 all-gather.4.cloned.1.call-start
  8.1 0.7 all-gather.4.cloned.1.call-update
  8.7 0.0 reduce-scatter.5.cloned.1.call-start
  8.8 1.1 broadcast_in_dim.2
  9.9 37.6 %all_to_all.38 = bf16[16,128,512]{2,1,0:T(8,128)(2,1)S(1)} all-to-all(bf16[16,128,512]{2,1,0:T(8,128)(2,1)S(1)} %broadcast_in_dim.2), channel_id=1, replica_groups=mesh['row'=16,'col'=8] {'row'}, dimensions={0} | all-to-all | bytes 4194304 | tf_op jit(solution)/shard_map/all_to_all | solution.py:21
  47.5 0.0 copy-start.1
  47.5 1.4 copy-done.1
  48.9 0.0 copy-done
  48.9 4.3 %convolution_convert_fusion = bf16[2048,1024]{1,0:T(8,128)(2,1)} fusion(bf16[2048,512]{1,0:T(8,128)(2,1)S(1)} %bitcast.21, bf16[1024,512]{1,0:T(8,128)(2,1)S(1)} %copy-done), kind=kOutput, calls=%fused_computation.2 | convolution fusion | flops 2149580800 | bytes 7340032 | tf_op jit(solution)/shard_map/dot_general | solution.py:29
  53.2 0.0 copy-start.4
  53.2 0.0 reduce-scatter.5.cloned.1.call-update
  53.3 0.0 reduce-scatter.3.cloned.1.call-start
  53.3 12.5 %all-gather.4.cloned.1.call-done = bf16[2048,512]{1,0:T(8,128)(2,1)} async-done(((bf16[128,512]{1,0:T(8,128)(2,1)}), bf16[2048,512]{1,0:T(8,128)(2,1)}) %all-gather.4.cloned.1.call-update) | async-done | bytes 2097168 | tf_op jit(solution)/shard_map/all_gather | solution.py:14
  65.8 0.0 copy-done.4
  65.8 5.9 %convolution_convert_fusion.1 = bf16[2048,1024]{1,0:T(8,128)(2,1)} fusion(bf16[2048,512]{1,0:T(8,128)(2,1)} %all-gather.4.cloned.1.call-done, bf16[512,1024]{1,0:T(8,128)(2,1)S(1)} %copy-done.4), kind=kOutput, calls=%fused_computation.3 | convolution fusion | flops 2149580800 | bytes 7340032 | tf_op jit(solution)/shard_map/dot_general | solution.py:38
  71.8 0.0 reduce-scatter.3.cloned.1.call-update
  71.8 0.0 all-gather.6.cloned.1.call-start
  71.9 15.8 %reduce-scatter.5.cloned.1.call-done = bf16[256,1024]{1,0:T(8,128)(2,1)} async-done(((bf16[2048,1024]{1,0:T(8,128)(2,1)}), bf16[256,1024]{1,0:T(8,128)(2,1)}) %reduce-scatter.5.cloned.1.call-update) | async-done | bytes 524304 | tf_op jit(solution)/shard_map/reduce_scatter | solution.py:39
  87.7 38.8 %reduce-scatter.3.cloned.1.call-done = bf16[256,1024]{1,0:T(8,128)(2,1)} async-done(((bf16[2048,1024]{1,0:T(8,128)(2,1)}), bf16[256,1024]{1,0:T(8,128)(2,1)}) %reduce-scatter.3.cloned.1.call-update) | async-done | bytes 524304 | tf_op jit(solution)/shard_map/reduce_scatter | solution.py:39
  126.4 4.6 %fusion.38 = (bf16[256,1024]{1,0:T(8,128)(2,1)}, bf16[256,1024]{1,0:T(8,128)(2,1)}) fusion(bf16[256,1024]{1,0:T(8,128)(2,1)} %reduce-scatter.3.cloned.1.call-done, bf16[256,1024]{1,0:T(8,128)(2,1)} %reduce-scatter.5.cloned.1.call-done), kind=kLoop, calls=%fused_computation.52 | loop fusion | flops 20185088 | bytes 2097152 | tf_op jit(solution)/shard_map/convert_element_type | solution.py:61
  131.0 0.0 all-gather.6.cloned.1.call-update
  131.0 0.0 all-gather.8.cloned.1.call-start
  131.1 0.7 all-gather.8.cloned.1.call-update
  131.8 33.5 %all-gather.6.cloned.1.call-done = bf16[2048,1024]{1,0:T(8,128)(2,1)} async-done(((bf16[256,1024]{1,0:T(8,128)(2,1)}), bf16[2048,1024]{1,0:T(8,128)(2,1)}) %all-gather.6.cloned.1.call-update) | async-done | bytes 4194320 | tf_op jit(solution)/shard_map/all_gather | solution.py:25
  165.3 5.8 %convolution_convert_fusion.3 = bf16[2048,512]{1,0:T(8,128)(2,1)} fusion(bf16[2048,1024]{1,0:T(8,128)(2,1)} %all-gather.6.cloned.1.call-done, bf16[1024,512]{1,0:T(8,128)(2,1)S(1)} %copy-done), kind=kOutput, calls=%fused_computation.5 | convolution fusion | flops 2148532224 | bytes 7340032 | tf_op jit(solution)/shard_map/dot_general | solution.py:49
  171.1 6.7 %all-to-all-start = ((bf16[16,128,512]{2,1,0:T(8,128)(2,1)}), bf16[16,128,512]{2,1,0:T(8,128)(2,1)S(1)}, u32[]{:S(2)}, u32[]{:S(2)}) async-start(bf16[16,128,512]{2,1,0:T(8,128)(2,1)} %bitcast.24), calls=%async_computation.1 | async-start | bytes 4194304 | tf_op jit(solution)/shard_map/all_to_all | solution.py:51
  177.9 21.7 %all-gather.8.cloned.1.call-done = bf16[2048,1024]{1,0:T(8,128)(2,1)} async-done(((bf16[256,1024]{1,0:T(8,128)(2,1)}), bf16[2048,1024]{1,0:T(8,128)(2,1)}) %all-gather.8.cloned.1.call-update) | async-done | bytes 4194320 | tf_op jit(solution)/shard_map/all_gather | solution.py:25
  199.5 6.2 %convolution_convert_fusion.2 = bf16[2048,512]{1,0:T(8,128)(2,1)} fusion(bf16[2048,1024]{1,0:T(8,128)(2,1)} %all-gather.8.cloned.1.call-done, bf16[512,1024]{1,0:T(8,128)(2,1)} %param.5), kind=kOutput, calls=%fused_computation.4 | convolution fusion | flops 2148532224 | bytes 7340032 | tf_op jit(solution)/shard_map/dot_general | solution.py:29
  205.7 1.4 all-to-all-done
  207.1 5.4 %all-to-all-start.3 = ((bf16[16,128,512]{2,1,0:T(8,128)(2,1)}), bf16[16,128,512]{2,1,0:T(8,128)(2,1)}, u32[]{:S(2)}, u32[]{:S(2)}) async-start(bf16[16,128,512]{2,1,0:T(8,128)(2,1)} %bitcast.23), calls=%async_computation.5 | async-start | bytes 4194304 | tf_op jit(solution)/shard_map/all_to_all | solution.py:51
  212.5 6.6 %convolution_bitcast_fusion = f32[512,1024]{0,1:T(8,128)} fusion(bf16[2048,1024]{1,0:T(8,128)(2,1)} %all-gather.8.cloned.1.call-done, bf16[2048,512]{1,0:T(8,128)(2,1)} %all-gather.4.cloned.1.call-done), kind=kOutput, calls=%fused_computation.12 | convolution fusion | flops 2147483648 | bytes 8388608 | tf_op jit(solution)/shard_map/dot_general | solution.py:68
  219.0 2.9 %copy.12 = f32[512,1024]{1,0:T(8,128)} copy(f32[512,1024]{0,1:T(8,128)} %convolution_bitcast_fusion) | data formatting | bytes 4194304
  221.9 6.5 %fusion.39 = f32[1024,512]{1,0:T(8,128)} fusion(bf16[2048,1024]{1,0:T(8,128)(2,1)} %all-gather.6.cloned.1.call-done, bf16[2048,512]{1,0:T(8,128)(2,1)} %bitcast.22), kind=kOutput, calls=%fused_computation.55 | convolution fusion | flops 2147483648 | bytes 8388608 | tf_op jit(solution)/shard_map/dot_general | solution.py:65
  228.5 0.0 copy-start.3
  228.5 0.3 convert_reduce_fusion.1
  228.8 0.6 copy-done.3
  229.4 0.0 copy-start.2
  229.4 0.7 add_convert_fusion.1
  230.0 8.0 %all-to-all-done.3 = bf16[16,128,512]{2,1,0:T(8,128)(2,1)} async-done(((bf16[16,128,512]{2,1,0:T(8,128)(2,1)}), bf16[16,128,512]{2,1,0:T(8,128)(2,1)}, u32[]{:S(2)}, u32[]{:S(2)}) %all-to-all-start.3) | async-done | bytes 2097184 | tf_op jit(solution)/shard_map/all_to_all | solution.py:51
  238.1 8.6 %all-to-all-start.1 = ((bf16[8,16,512]{2,1,0:T(8,128)(2,1)}), bf16[8,16,512]{2,1,0:T(8,128)(2,1)S(1)}, u32[]{:S(2)}, u32[]{:S(2)}) async-start(bf16[8,16,512]{2,1,0:T(8,128)(2,1)} %bitcast.1), calls=%async_computation.2 | async-start | bytes 262144 | tf_op jit(solution)/shard_map/all_to_all | solution.py:64
  246.7 1.9 convert_reduce_fusion
  248.6 0.0 copy-done.2
  248.6 0.7 add_convert_fusion
  249.3 2.7 %all-to-all-done.1 = bf16[8,16,512]{2,1,0:T(8,128)(2,1)S(1)} async-done(((bf16[8,16,512]{2,1,0:T(8,128)(2,1)}), bf16[8,16,512]{2,1,0:T(8,128)(2,1)S(1)}, u32[]{:S(2)}, u32[]{:S(2)}) %all-to-all-start.1) | async-done | bytes 131104 | tf_op jit(solution)/shard_map/all_to_all | solution.py:64
  252.0 0.7 copy.13
Async XLA Ops:
  8.0 40.9 %copy-start = (bf16[1024,512]{1,0:T(8,128)(2,1)S(1)}, bf16[1024,512]{1,0:T(8,128)(2,1)}, u32[]{:S(2)}) copy-start(bf16[1024,512]{1,0:T(8,128)(2,1)} %param.6) | copy-start | bytes 3145732
  8.0 57.8 %all-gather.4.cloned.1.call-start = ((), (), s32[]{:S(2)}) async-start(), calls=%async_computation.6 | async-start | bytes 2228224 | tf_op jit(solution)/shard_map/all_gather | solution.py:14
  8.7 78.9 %reduce-scatter.5.cloned.1.call-start = ((), (), s32[]{:S(2)}) async-start(), calls=%async_computation.9 | async-start | bytes 4718592 | tf_op jit(solution)/shard_map/reduce_scatter | solution.py:39
  47.5 1.4 copy-start.1
  53.2 12.6 %copy-start.4 = (bf16[512,1024]{1,0:T(8,128)(2,1)S(1)}, bf16[512,1024]{1,0:T(8,128)(2,1)}, u32[]{:S(2)}) copy-start(bf16[512,1024]{1,0:T(8,128)(2,1)} %param.5) | copy-start | bytes 3145732
  53.3 73.2 %reduce-scatter.3.cloned.1.call-start = ((), (), s32[]{:S(2)}) async-start(), calls=%async_computation.7 | async-start | bytes 4718592 | tf_op jit(solution)/shard_map/reduce_scatter | solution.py:39
  71.8 93.5 %all-gather.6.cloned.1.call-start = ((), (), s32[]{:S(2)}) async-start(), calls=%async_computation.8 | async-start | bytes 4718592 | tf_op jit(solution)/shard_map/all_gather | solution.py:25
  131.0 68.5 %all-gather.8.cloned.1.call-start = ((), (), s32[]{:S(2)}) async-start(), calls=%async_computation.10 | async-start | bytes 4718592 | tf_op jit(solution)/shard_map/all_gather | solution.py:25
  171.1 35.9 %all-to-all-start = ((bf16[16,128,512]{2,1,0:T(8,128)(2,1)}), bf16[16,128,512]{2,1,0:T(8,128)(2,1)S(1)}, u32[]{:S(2)}, u32[]{:S(2)}) async-start(bf16[16,128,512]{2,1,0:T(8,128)(2,1)} %bitcast.24), calls=%async_computation.1 | async-start | bytes 4194304 | tf_op jit(solution)/shard_map/all_to_all | solution.py:51
  207.1 31.0 %all-to-all-start.3 = ((bf16[16,128,512]{2,1,0:T(8,128)(2,1)}), bf16[16,128,512]{2,1,0:T(8,128)(2,1)}, u32[]{:S(2)}, u32[]{:S(2)}) async-start(bf16[16,128,512]{2,1,0:T(8,128)(2,1)} %bitcast.23), calls=%async_computation.5 | async-start | bytes 4194304 | tf_op jit(solution)/shard_map/all_to_all | solution.py:51
  228.5 0.9 copy-start.3
  229.4 19.2 %copy-start.2 = (bf16[128,512]{1,0:T(8,128)(2,1)S(1)}, bf16[128,512]{1,0:T(8,128)(2,1)}, u32[]{:S(2)}) copy-start(bf16[128,512]{1,0:T(8,128)(2,1)} %param.7) | copy-start | bytes 393220
  238.1 13.9 %all-to-all-start.1 = ((bf16[8,16,512]{2,1,0:T(8,128)(2,1)}), bf16[8,16,512]{2,1,0:T(8,128)(2,1)S(1)}, u32[]{:S(2)}, u32[]{:S(2)}) async-start(bf16[8,16,512]{2,1,0:T(8,128)(2,1)} %bitcast.1), calls=%async_computation.2 | async-start | bytes 262144 | tf_op jit(solution)/shard_map/all_to_all | solution.py:64
Sparse Core Ops, SparseCore 0:
  11.0 54.8 all-gather.3
Sparse Core Ops, SparseCore 1:
  53.4 34.3 reduce-scatter.4
  89.9 36.4 reduce-scatter.2
  131.1 34.1 all-gather.5
  167.6 31.9 all-gather.7
where the time goes:
time: 261 us; the launch traced here: 260 us
  waiting for transfers between devices  136 us (52%)
  blocking collectives  37.6 us (14%)
  matrix products  35.4 us (14%)
  starting transfers between devices  20.9 us (8%)
  between operations  15.7 us (6%)
  other arithmetic  8.13 us (3%)
  local copies, waits for them, and re-layouts  6.64 us (3%)
    all_gather x2, waiting for transfers between devices, hidden_panel(): return lax.all_gather(local_rows, 'col', axis=0, tiled=True)  55.2 us
    reduce_scatter x2, waiting for transfers between devices, width_split(): lax.psum_scatter(term.astype(jnp.bfloat16), 'col', scatter_dimension=0, t...  54.6 us
    all_to_all x1, blocking collectives, token_panel_a2a(): lax.all_to_all(copies, 'row', split_axis=0, concat_axis=0, tiled=True)  37.6 us
    all_gather x1, waiting for transfers between devices, token_panel(): return lax.all_gather(local_rows, 'row', axis=0, tiled=True)  12.5 us
    all_to_all x2, starting transfers between devices, unit_sum(): lax.all_to_all(pieces, 'row', split_axis=0, concat_axis=0, tiled=True)  12.1 us
    dot_general x2, matrix products, contract_last(): lax.dot_general(left, right, (((1,), (1,)), ((), ())), preferred_element_...  10.5 us
    all_to_all x2, waiting for transfers between devices, unit_sum(): lax.all_to_all(pieces, 'row', split_axis=0, concat_axis=0, tiled=True)  9.4 us
    all_to_all x1, starting transfers between devices, local(): lax.all_to_all(block_rows, 'col', split_axis=0, concat_axis=1, tiled=True)  8.57 us
  transfers between devices with their start and end apart: 8, of which 8 were waited for; matrix products, arithmetic and copies ran while one was open for 17% of the time, Pallas kernels for 0%

commit v1 on v0

--- a/solution.py
+++ b/solution.py
@@ -1,7 +1,33 @@
+import functools
 import jax
 import jax.numpy as jnp
 from jax import lax
 from jax.sharding import PartitionSpec as P
+from jax.lax import axis_index, axis_size, ppermute
+
+
+def solve_the_target(payload, along_axis):
+    block_now = axis_size(along_axis)
+    q_next = axis_index(along_axis)
+    o_now, b_now, current_block = (block_now, q_next, payload.shape[0])
+    views = [w * o_now if jj == 0 else w for jj, w in enumerate(payload.shape)]
+    z_new = jnp.zeros(views, payload.dtype)
+    base_arr = lax.dynamic_update_slice_in_dim(z_new, payload, b_now * current_block, axis=0)
+    new = shaped = payload
+    for q in range(1, o_now // 2 + 1):
+        new = ppermute(new, along_axis, [(jj, (jj + 1) % o_now) for jj in range(o_now)])
+        base_arr = lax.dynamic_update_slice_in_dim(
+            base_arr, new, (b_now - q) % o_now * current_block, axis=0
+        )
+        if 2 * q < o_now:
+            shaped = ppermute(shaped, along_axis, [(jj, (jj - 1) % o_now) for jj in range(o_now)])
+            base_arr = lax.dynamic_update_slice_in_dim(
+                base_arr, shaped, (b_now + q) % o_now * current_block, axis=0
+            )
+    return base_arr
+
+
+stops_all_plan = functools.partial(solve_the_target, along_axis="col")
 
 
 def gelu_grad(value):
@@ -22,7 +48,7 @@
 
 
 def hidden_panel(local_rows):
-    return lax.all_gather(local_rows, "col", axis=0, tiled=True)
+    return stops_all_plan(local_rows)
 
 
 def contract_last(left, right):

time: 261 us -> 272 us (1.042)
  waiting for transfers between devices: 136 us -> 97.4 us
  starting transfers between devices: 20.9 us -> 56.7 us
  local copies, waits for them, and re-layouts: 6.64 us -> 28.9 us
  blocking collectives: 37.6 us -> 30.7 us
    all_gather x2 -> x0, waiting for transfers between devices: 55.2 us -> none  [hidden_panel(): return lax.all_gather(local_rows, 'col', axis=0, tiled=True)]
    all_gather x1, waiting for transfers between devices: 12.5 us -> 49.7 us  [token_panel(): return lax.all_gather(local_rows, 'row', axis=0, tiled=True)]
    reduce_scatter x2, waiting for transfers between devices: 54.6 us -> 22.3 us  [width_split(): lax.psum_scatter(term.astype(jnp.bfloat16), 'col', scatter_dimension=0, t...]
    ppermute x0 -> x14, starting transfers between devices: none -> 26.6 us  [the longest x8 14.7 us: solve_the_target(): ppermute(new, along_axis, [(jj, (jj + 1) % o_now) for jj in range(o_now)])]
    ppermute x0 -> x14, waiting for transfers between devices: none -> 20.3 us  [the longest x8 13.2 us: solve_the_target(): ppermute(new, along_axis, [(jj, (jj + 1) % o_now) for jj in range(o_now)])]
    dynamic_update_slice x0 -> x14, local copies, waits for them, and re-layouts: none -> 18 us  [the longest x8 10.9 us: solve_the_target(): lax.dynamic_update_slice_in_dim(base_arr, new, (b_now - q) % o_now * curr...]
    all_to_all x1, starting transfers between devices: 8.57 us -> 18.8 us  [local(): lax.all_to_all(block_rows, 'col', split_axis=0, concat_axis=1, tiled=True)]
    all_to_all x2, waiting for transfers between devices: 9.4 us -> 1.73 us  [unit_sum(): lax.all_to_all(pieces, 'row', split_axis=0, concat_axis=0, tiled=True)]
  transfers between devices with their start and end apart: 8 -> 20, of which waited for: 8 -> 10; matrix products, arithmetic and copies ran while one was open for 17% -> 23% of each run, Pallas kernels for 0% -> 0%
where the time goes in v1:
time: 272 us; the launch traced here: 271 us
  waiting for transfers between devices  97.4 us (36%)
  starting transfers between devices  56.7 us (21%)
  matrix products  35.4 us (13%)
  blocking collectives  30.7 us (11%)
  local copies, waits for them, and re-layouts  28.9 us (11%)
  between operations  13.9 us (5%)
  other arithmetic  7.88 us (3%)
    all_gather x1, waiting for transfers between devices, token_panel(): return lax.all_gather(local_rows, 'row', axis=0, tiled=True)  49.7 us
    all_to_all x1, blocking collectives, token_panel_a2a(): lax.all_to_all(copies, 'row', split_axis=0, concat_axis=0, tiled=True)  30.7 us
    reduce_scatter x2, waiting for transfers between devices, width_split(): lax.psum_scatter(term.astype(jnp.bfloat16), 'col', scatter_dimension=0, t...  22.3 us
    all_to_all x1, starting transfers between devices, local(): lax.all_to_all(block_rows, 'col', split_axis=0, concat_axis=1, tiled=True)  18.8 us
    ppermute x8, starting transfers between devices, solve_the_target(): ppermute(new, along_axis, [(jj, (jj + 1) % o_now) for jj in range(o_now)])  14.7 us
    ppermute x8, waiting for transfers between devices, solve_the_target(): ppermute(new, along_axis, [(jj, (jj + 1) % o_now) for jj in range(o_now)])  13.2 us
    ppermute x6, starting transfers between devices, solve_the_target(): ppermute(shaped, along_axis, [(jj, (jj - 1) % o_now) for jj in range(o_no...  11.9 us
    all_to_all x2, starting transfers between devices, unit_sum(): lax.all_to_all(pieces, 'row', split_axis=0, concat_axis=0, tiled=True)  11.1 us
  transfers between devices with their start and end apart: 20, of which 10 were waited for; matrix products, arithmetic and copies ran while one was open for 23% of the time, Pallas kernels for 0%

profile of v1, /device:TPU:1, one launch (start us, length us, event | category | flops | bytes accessed | tf_op | source)
XLA Modules:
  0.0 270.8 jit_solution(1200020371998142489)
XLA Ops:
  8.0 49.7 %all-gather.2.cloned.1.call-done = bf16[2048,512]{1,0:T(8,128)(2,1)} async-done(((bf16[128,512]{1,0:T(8,128)(2,1)}), bf16[2048,512]{1,0:T(8,128)(2,1)}) %all-gather.2.cloned.1.call-update) | async-done | bytes 2097168 | tf_op jit(solution)/shard_map/all_gather | solution.py:40
  57.6 6.2 %convolution_convert_fusion.1 = bf16[2048,1024]{1,0:T(8,128)(2,1)} fusion(bf16[2048,512]{1,0:T(8,128)(2,1)} %all-gather.2.cloned.1.call-done, bf16[512,1024]{1,0:T(8,128)(2,1)} %param.5), kind=kOutput, calls=%fused_computation.3 | convolution fusion | flops 2149580800 | bytes 7340032 | tf_op jit(solution)/shard_map/dot_general | solution.py:64
  65.0 30.7 %all_to_all.38 = bf16[16,128,512]{2,1,0:T(8,128)(2,1)S(1)} all-to-all(bf16[16,128,512]{2,1,0:T(8,128)(2,1)S(1)} %broadcast_in_dim.2), channel_id=1, replica_groups=mesh['row'=16,'col'=8] {'row'}, dimensions={0} | all-to-all | bytes 4194304 | tf_op jit(solution)/shard_map/all_to_all | solution.py:47
  95.6 1.3 copy-done.1
  97.0 4.3 %convolution_convert_fusion = bf16[2048,1024]{1,0:T(8,128)(2,1)} fusion(bf16[2048,512]{1,0:T(8,128)(2,1)S(1)} %bitcast.21, bf16[1024,512]{1,0:T(8,128)(2,1)S(1)} %copy-done), kind=kOutput, calls=%fused_computation.2 | convolution fusion | flops 2149580800 | bytes 7340032 | tf_op jit(solution)/shard_map/dot_general | solution.py:55
  101.4 2.6 broadcast.20.clone
  103.9 3.0 %constant_dynamic-update-slice_fusion.15 = (bf16[2048,1024]{1,0:T(8,128)(2,1)}, bf16[256,1024]{1,0:T(8,128)(2,1)S(1)}) fusion(bf16[2048,1024]{1,0:T(8,128)(2,1)} %broadcast.20.clone, s32[]{:T(128)S(6)} %select_n.77, bf16[256,1024]{1,0:T(8,128)(2,1)S(1)} %copy-done.2), kind=kLoop, calls=%fused_computation.70 | loop fusion | flops 17301504 | bytes 1572868 | tf_op jit(solution)/shard_map/dynamic_update_slice | solution.py:15
  106.9 4.2 %collective-permute-start = (bf16[256,1024]{1,0:T(8,128)(2,1)S(1)}, bf16[256,1024]{1,0:T(8,128)(2,1)}, u32[]{:S(2)}, u32[]{:S(2)}) collective-permute-start(bf16[256,1024]{1,0:T(8,128)(2,1)S(1)} %get-tuple-element.19), channel_id=1, source_target_pairs={{0,1},{1,2},{2,3},{3,4},{4,5},{5,6},{6,7},{7,0},{8,9},{9,10},{10,1... | collective-permute-start | bytes 1572872 | tf_op jit(solution)/shard_map/ppermute | solution.py:18
  111.1 10.8 %collective-permute-done = bf16[256,1024]{1,0:T(8,128)(2,1)} collective-permute-done((bf16[256,1024]{1,0:T(8,128)(2,1)S(1)}, bf16[256,1024]{1,0:T(8,128)(2,1)}, u32[]{:S(2)}, u32[]{:S(2)}) %collective-permute-start) | collective-permute-done | bytes 524320 | tf_op jit(solution)/shard_map/ppermute | solution.py:18
  121.9 2.6 collective-permute-start.2
  124.5 22.3 %reduce-scatter.5.cloned.1.call-done = bf16[256,1024]{1,0:T(8,128)(2,1)} async-done(((bf16[2048,1024]{1,0:T(8,128)(2,1)}), bf16[256,1024]{1,0:T(8,128)(2,1)}) %reduce-scatter.5.cloned.1.call-update) | async-done | bytes 524304 | tf_op jit(solution)/shard_map/reduce_scatter | solution.py:65
  146.8 2.5 broadcast.20.clone.1
  149.2 1.3 constant_dynamic-update-slice_fusion.7
  150.5 1.3 collective-permute-start.7
  151.8 1.0 collective-permute-start.8
  152.8 3.0 %collective-permute-start.3 = (bf16[256,1024]{1,0:T(8,128)(2,1)S(1)}, bf16[256,1024]{1,0:T(8,128)(2,1)S(1)}, u32[]{:S(2)}, u32[]{:S(2)}) collective-permute-start(bf16[256,1024]{1,0:T(8,128)(2,1)S(1)} %collective-permute-done.1), channel_id=1, source_target_pairs={{0,7},{1,0},{2,1},{3,2},{4,3},{5,4},{6,5},{7,6},{8,15},{9,8},{10,9... | collective-permute-start | bytes 1572872 | tf_op jit(solution)/shard_map/ppermute | solution.py:23
  155.7 2.2 collective-permute-done.7
  157.9 2.6 collective-permute-start.9
  160.8 1.9 collective-permute-start.10
  162.7 3.6 %collective-permute-done.3 = bf16[256,1024]{1,0:T(8,128)(2,1)S(1)} collective-permute-done((bf16[256,1024]{1,0:T(8,128)(2,1)S(1)}, bf16[256,1024]{1,0:T(8,128)(2,1)S(1)}, u32[]{:S(2)}, u32[]{:S(2)}) %collective-permute-start.3) | collective-permute-done | bytes 524320 | tf_op jit(solution)/shard_map/ppermute | solution.py:23
  166.3 1.7 collective-permute-start.5
  168.0 1.9 constant_dynamic-update-slice_fusion.14
  170.0 0.8 constant_dynamic-update-slice_fusion.13
  170.8 1.9 constant_dynamic-update-slice_fusion.12
  172.7 0.8 constant_dynamic-update-slice_fusion.11
  173.6 0.8 constant_dynamic-update-slice_fusion.10
  174.4 3.2 %collective-permute-done.5 = bf16[256,1024]{1,0:T(8,128)(2,1)S(1)} collective-permute-done((bf16[256,1024]{1,0:T(8,128)(2,1)S(1)}, bf16[256,1024]{1,0:T(8,128)(2,1)S(1)}, u32[]{:S(2)}, u32[]{:S(2)}) %collective-permute-start.5) | collective-permute-done | bytes 524320 | tf_op jit(solution)/shard_map/ppermute | solution.py:23
  177.6 0.8 constant_dynamic-update-slice_fusion.9
  179.2 5.8 %convolution_convert_fusion.3 = bf16[2048,512]{1,0:T(8,128)(2,1)} fusion(bf16[2048,1024]{1,0:T(8,128)(2,1)} %constant_dynamic-update-slice_fusion.8, bf16[1024,512]{1,0:T(8,128)(2,1)S(1)} %copy-done), kind=kOutput, calls=%fused_computation.5 | convolution fusion | flops 2148532224 | bytes 7340032 | tf_op jit(solution)/shard_map/dot_general | solution.py:75
  185.1 4.1 %all-to-all-start = ((bf16[16,128,512]{2,1,0:T(8,128)(2,1)}), bf16[16,128,512]{2,1,0:T(8,128)(2,1)S(1)}, u32[]{:S(2)}, u32[]{:S(2)}) async-start(bf16[16,128,512]{2,1,0:T(8,128)(2,1)} %bitcast.23), calls=%async_computation.1 | async-start | bytes 4194304 | tf_op jit(solution)/shard_map/all_to_all | solution.py:77
  189.2 1.7 collective-permute-start.11
  190.9 4.4 %collective-permute-start.12 = (bf16[256,1024]{1,0:T(8,128)(2,1)}, bf16[256,1024]{1,0:T(8,128)(2,1)S(1)}, u32[]{:S(2)}, u32[]{:S(2)}) collective-permute-start(bf16[256,1024]{1,0:T(8,128)(2,1)} %collective-permute-done.10), channel_id=1, source_target_pairs={{0,7},{1,0},{2,1},{3,2},{4,3},{5,4},{6,5},{7,6},{8,15},{9,8},{10,9... | collective-permute-start | bytes 1572872 | tf_op jit(solution)/shard_map/ppermute | solution.py:23
  195.4 1.9 constant_dynamic-update-slice_fusion.6
  197.4 2.4 collective-permute-start.13
  199.7 1.9 constant_dynamic-update-slice_fusion.5
  201.6 1.9 constant_dynamic-update-slice_fusion.4
  203.5 1.9 constant_dynamic-update-slice_fusion.3
  205.4 0.8 constant_dynamic-update-slice_fusion.2
  206.2 0.8 constant_dynamic-update-slice_fusion.1
  207.9 5.9 %convolution_convert_fusion.2 = bf16[2048,512]{1,0:T(8,128)(2,1)} fusion(bf16[2048,1024]{1,0:T(8,128)(2,1)} %constant_dynamic-update-slice_fusion, bf16[512,1024]{1,0:T(8,128)(2,1)S(1)} %copy-done.6), kind=kOutput, calls=%fused_computation.4 | convolution fusion | flops 2148532224 | bytes 7340032 | tf_op jit(solution)/shard_map/dot_general | solution.py:55
  213.8 7.0 %all-to-all-start.3 = ((bf16[16,128,512]{2,1,0:T(8,128)(2,1)}), bf16[16,128,512]{2,1,0:T(8,128)(2,1)}, u32[]{:S(2)}, u32[]{:S(2)}) async-start(bf16[16,128,512]{2,1,0:T(8,128)(2,1)} %bitcast.24), calls=%async_computation.5 | async-start | bytes 4194304 | tf_op jit(solution)/shard_map/all_to_all | solution.py:77
  220.8 6.5 %convolution_bitcast_fusion = f32[512,1024]{0,1:T(8,128)} fusion(bf16[2048,1024]{1,0:T(8,128)(2,1)} %constant_dynamic-update-slice_fusion, bf16[2048,512]{1,0:T(8,128)(2,1)} %all-gather.2.cloned.1.call-done), kind=kOutput, calls=%fused_computation.12 | convolution fusion | flops 2147483648 | bytes 8388608 | tf_op jit(solution)/shard_map/dot_general | solution.py:94
  227.3 2.9 %copy.12 = f32[512,1024]{1,0:T(8,128)} copy(f32[512,1024]{0,1:T(8,128)} %convolution_bitcast_fusion) | data formatting | bytes 4194304
  230.2 6.6 %fusion.41 = f32[1024,512]{1,0:T(8,128)} fusion(bf16[2048,1024]{1,0:T(8,128)(2,1)} %constant_dynamic-update-slice_fusion.8, bf16[2048,512]{1,0:T(8,128)(2,1)} %bitcast.22), kind=kOutput, calls=%fused_computation.71 | convolution fusion | flops 2147483648 | bytes 8388608 | tf_op jit(solution)/shard_map/dot_general | solution.py:91
  237.8 1.7 all-to-all-done.3
  239.5 18.8 %all-to-all-start.1 = ((bf16[8,16,512]{2,1,0:T(8,128)(2,1)}), bf16[8,16,512]{2,1,0:T(8,128)(2,1)S(1)}, u32[]{:S(2)}, u32[]{:S(2)}) async-start(bf16[8,16,512]{2,1,0:T(8,128)(2,1)} %bitcast.1), calls=%async_computation.2 | async-start | bytes 262144 | tf_op jit(solution)/shard_map/all_to_all | solution.py:90
  258.3 1.9 convert_reduce_fusion
  260.9 2.7 all-to-all-done.1
  (41 shorter events, 6.4 us)
Async XLA Ops:
  7.2 89.8 %copy-start = (bf16[1024,512]{1,0:T(8,128)(2,1)S(1)}, bf16[1024,512]{1,0:T(8,128)(2,1)}, u32[]{:S(2)}) copy-start(bf16[1024,512]{1,0:T(8,128)(2,1)} %param.6) | copy-start | bytes 3145732
  7.2 50.5 %all-gather.2.cloned.1.call-start = ((), (), s32[]{:S(2)}) async-start(), calls=%async_computation.6 | async-start | bytes 2228224 | tf_op jit(solution)/shard_map/all_gather | solution.py:40
  7.9 93.4 %reduce-scatter.3.cloned.1.call-start = ((), (), s32[]{:S(2)}) async-start(), calls=%async_computation.7 | async-start | bytes 4718592 | tf_op jit(solution)/shard_map/reduce_scatter | solution.py:65
  63.9 0.9 copy-start.4
  63.9 82.9 %reduce-scatter.5.cloned.1.call-start = ((), (), s32[]{:S(2)}) async-start(), calls=%async_computation.8 | async-start | bytes 4718592 | tf_op jit(solution)/shard_map/reduce_scatter | solution.py:65
  95.6 1.3 copy-start.1
  101.4 2.6 copy-start.2
  106.9 15.0 %collective-permute-start = (bf16[256,1024]{1,0:T(8,128)(2,1)S(1)}, bf16[256,1024]{1,0:T(8,128)(2,1)}, u32[]{:S(2)}, u32[]{:S(2)}) collective-permute-start(bf16[256,1024]{1,0:T(8,128)(2,1)S(1)} %get-tuple-element.19), channel_id=1, source_target_pairs={{0,1},{1,2},{2,3},{3,4},{4,5},{5,6},{6,7},{7,0},{8,9},{9,10},{10,1... | collective-permute-start | bytes 1572872 | tf_op jit(solution)/shard_map/ppermute | solution.py:18
  111.1 41.7 %collective-permute-start.1 = (bf16[256,1024]{1,0:T(8,128)(2,1)S(1)}, bf16[256,1024]{1,0:T(8,128)(2,1)S(1)}, u32[]{:S(2)}, u32[]{:S(2)}) collective-permute-start(bf16[256,1024]{1,0:T(8,128)(2,1)S(1)} %get-tuple-element.19), channel_id=1, source_target_pairs={{0,7},{1,0},{2,1},{3,2},{4,3},{5,4},{6,5},{7,6},{8,15},{9,8},{10,9... | collective-permute-start | bytes 1572872 | tf_op jit(solution)/shard_map/ppermute | solution.py:23
  121.9 33.8 %collective-permute-start.2 = (bf16[256,1024]{1,0:T(8,128)(2,1)}, bf16[256,1024]{1,0:T(8,128)(2,1)}, u32[]{:S(2)}, u32[]{:S(2)}) collective-permute-start(bf16[256,1024]{1,0:T(8,128)(2,1)} %collective-permute-done), channel_id=1, source_target_pairs={{0,1},{1,2},{2,3},{3,4},{4,5},{5,6},{6,7},{7,0},{8,9},{9,10},{10,1... | collective-permute-start | bytes 1572872 | tf_op jit(solution)/shard_map/ppermute | solution.py:18
  146.8 2.5 copy-start.3
  150.5 7.4 %collective-permute-start.7 = (bf16[256,1024]{1,0:T(8,128)(2,1)S(1)}, bf16[256,1024]{1,0:T(8,128)(2,1)}, u32[]{:S(2)}, u32[]{:S(2)}) collective-permute-start(bf16[256,1024]{1,0:T(8,128)(2,1)S(1)} %get-tuple-element.17), channel_id=1, source_target_pairs={{0,1},{1,2},{2,3},{3,4},{4,5},{5,6},{6,7},{7,0},{8,9},{9,10},{10,1... | collective-permute-start | bytes 1572872 | tf_op jit(solution)/shard_map/ppermute | solution.py:18
  151.8 9.0 %collective-permute-start.8 = (bf16[256,1024]{1,0:T(8,128)(2,1)S(1)}, bf16[256,1024]{1,0:T(8,128)(2,1)}, u32[]{:S(2)}, u32[]{:S(2)}) collective-permute-start(bf16[256,1024]{1,0:T(8,128)(2,1)S(1)} %get-tuple-element.17), channel_id=1, source_target_pairs={{0,7},{1,0},{2,1},{3,2},{4,3},{5,4},{6,5},{7,6},{8,15},{9,8},{10,9... | collective-permute-start | bytes 1572872 | tf_op jit(solution)/shard_map/ppermute | solution.py:23
  152.8 13.6 %collective-permute-start.3 = (bf16[256,1024]{1,0:T(8,128)(2,1)S(1)}, bf16[256,1024]{1,0:T(8,128)(2,1)S(1)}, u32[]{:S(2)}, u32[]{:S(2)}) collective-permute-start(bf16[256,1024]{1,0:T(8,128)(2,1)S(1)} %collective-permute-done.1), channel_id=1, source_target_pairs={{0,7},{1,0},{2,1},{3,2},{4,3},{5,4},{6,5},{7,6},{8,15},{9,8},{10,9... | collective-permute-start | bytes 1572872 | tf_op jit(solution)/shard_map/ppermute | solution.py:23
  155.7 14.2 %collective-permute-start.4 = (bf16[256,1024]{1,0:T(8,128)(2,1)}, bf16[256,1024]{1,0:T(8,128)(2,1)S(1)}, u32[]{:S(2)}, u32[]{:S(2)}) collective-permute-start(bf16[256,1024]{1,0:T(8,128)(2,1)} %collective-permute-done.2), channel_id=1, source_target_pairs={{0,1},{1,2},{2,3},{3,4},{4,5},{5,6},{6,7},{7,0},{8,9},{9,10},{10,1... | collective-permute-start | bytes 1572872 | tf_op jit(solution)/shard_map/ppermute | solution.py:18
  157.9 31.3 %collective-permute-start.9 = (bf16[256,1024]{1,0:T(8,128)(2,1)}, bf16[256,1024]{1,0:T(8,128)(2,1)}, u32[]{:S(2)}, u32[]{:S(2)}) collective-permute-start(bf16[256,1024]{1,0:T(8,128)(2,1)} %collective-permute-done.7), channel_id=1, source_target_pairs={{0,1},{1,2},{2,3},{3,4},{4,5},{5,6},{6,7},{7,0},{8,9},{9,10},{10,1... | collective-permute-start | bytes 1572872 | tf_op jit(solution)/shard_map/ppermute | solution.py:18
  160.8 30.1 %collective-permute-start.10 = (bf16[256,1024]{1,0:T(8,128)(2,1)}, bf16[256,1024]{1,0:T(8,128)(2,1)}, u32[]{:S(2)}, u32[]{:S(2)}) collective-permute-start(bf16[256,1024]{1,0:T(8,128)(2,1)} %collective-permute-done.8), channel_id=1, source_target_pairs={{0,7},{1,0},{2,1},{3,2},{4,3},{5,4},{6,5},{7,6},{8,15},{9,8},{10,9... | collective-permute-start | bytes 1572872 | tf_op jit(solution)/shard_map/ppermute | solution.py:23
  166.3 11.2 %collective-permute-start.5 = (bf16[256,1024]{1,0:T(8,128)(2,1)S(1)}, bf16[256,1024]{1,0:T(8,128)(2,1)S(1)}, u32[]{:S(2)}, u32[]{:S(2)}) collective-permute-start(bf16[256,1024]{1,0:T(8,128)(2,1)S(1)} %collective-permute-done.3), channel_id=1, source_target_pairs={{0,7},{1,0},{2,1},{3,2},{4,3},{5,4},{6,5},{7,6},{8,15},{9,8},{10,9... | collective-permute-start | bytes 1572872 | tf_op jit(solution)/shard_map/ppermute | solution.py:23
  169.9 8.5 %collective-permute-start.6 = (bf16[256,1024]{1,0:T(8,128)(2,1)S(1)}, bf16[256,1024]{1,0:T(8,128)(2,1)S(1)}, u32[]{:S(2)}, u32[]{:S(2)}) collective-permute-start(bf16[256,1024]{1,0:T(8,128)(2,1)S(1)} %collective-permute-done.4), channel_id=1, source_target_pairs={{0,1},{1,2},{2,3},{3,4},{4,5},{5,6},{6,7},{7,0},{8,9},{9,10},{10,1... | collective-permute-start | bytes 1572872 | tf_op jit(solution)/shard_map/ppermute | solution.py:18
  185.1 28.7 %all-to-all-start = ((bf16[16,128,512]{2,1,0:T(8,128)(2,1)}), bf16[16,128,512]{2,1,0:T(8,128)(2,1)S(1)}, u32[]{:S(2)}, u32[]{:S(2)}) async-start(bf16[16,128,512]{2,1,0:T(8,128)(2,1)} %bitcast.23), calls=%async_computation.1 | async-start | bytes 4194304 | tf_op jit(solution)/shard_map/all_to_all | solution.py:77
  189.2 18.7 %copy-start.6 = (bf16[512,1024]{1,0:T(8,128)(2,1)S(1)}, bf16[512,1024]{1,0:T(8,128)(2,1)}, u32[]{:S(2)}) copy-start(bf16[512,1024]{1,0:T(8,128)(2,1)} %param.5) | copy-start | bytes 3145732
  189.2 8.1 %collective-permute-start.11 = (bf16[256,1024]{1,0:T(8,128)(2,1)}, bf16[256,1024]{1,0:T(8,128)(2,1)S(1)}, u32[]{:S(2)}, u32[]{:S(2)}) collective-permute-start(bf16[256,1024]{1,0:T(8,128)(2,1)} %collective-permute-done.9), channel_id=1, source_target_pairs={{0,1},{1,2},{2,3},{3,4},{4,5},{5,6},{6,7},{7,0},{8,9},{9,10},{10,1... | collective-permute-start | bytes 1572872 | tf_op jit(solution)/shard_map/ppermute | solution.py:18
  190.9 15.3 %collective-permute-start.12 = (bf16[256,1024]{1,0:T(8,128)(2,1)}, bf16[256,1024]{1,0:T(8,128)(2,1)S(1)}, u32[]{:S(2)}, u32[]{:S(2)}) collective-permute-start(bf16[256,1024]{1,0:T(8,128)(2,1)} %collective-permute-done.10), channel_id=1, source_target_pairs={{0,7},{1,0},{2,1},{3,2},{4,3},{5,4},{6,5},{7,6},{8,15},{9,8},{10,9... | collective-permute-start | bytes 1572872 | tf_op jit(solution)/shard_map/ppermute | solution.py:23
  197.4 9.7 %collective-permute-start.13 = (bf16[256,1024]{1,0:T(8,128)(2,1)S(1)}, bf16[256,1024]{1,0:T(8,128)(2,1)S(1)}, u32[]{:S(2)}, u32[]{:S(2)}) collective-permute-start(bf16[256,1024]{1,0:T(8,128)(2,1)S(1)} %collective-permute-done.11), channel_id=1, source_target_pairs={{0,1},{1,2},{2,3},{3,4},{4,5},{5,6},{6,7},{7,0},{8,9},{9,10},{10,1... | collective-permute-start | bytes 1572872 | tf_op jit(solution)/shard_map/ppermute | solution.py:18
  213.8 25.7 %all-to-all-start.3 = ((bf16[16,128,512]{2,1,0:T(8,128)(2,1)}), bf16[16,128,512]{2,1,0:T(8,128)(2,1)}, u32[]{:S(2)}, u32[]{:S(2)}) async-start(bf16[16,128,512]{2,1,0:T(8,128)(2,1)} %bitcast.24), calls=%async_computation.5 | async-start | bytes 4194304 | tf_op jit(solution)/shard_map/all_to_all | solution.py:77
  230.2 6.9 %copy-start.5 = (bf16[128,512]{1,0:T(8,128)(2,1)S(1)}, bf16[128,512]{1,0:T(8,128)(2,1)}, u32[]{:S(2)}) copy-start(bf16[128,512]{1,0:T(8,128)(2,1)} %param.4) | copy-start | bytes 393220
  239.5 24.1 %all-to-all-start.1 = ((bf16[8,16,512]{2,1,0:T(8,128)(2,1)}), bf16[8,16,512]{2,1,0:T(8,128)(2,1)S(1)}, u32[]{:S(2)}, u32[]{:S(2)}) async-start(bf16[8,16,512]{2,1,0:T(8,128)(2,1)} %bitcast.1), calls=%async_computation.2 | async-start | bytes 262144 | tf_op jit(solution)/shard_map/all_to_all | solution.py:90
Sparse Core Ops, SparseCore 0:
  10.2 47.4 all-gather.1
  64.0 35.4 reduce-scatter.2
  101.9 44.7 reduce-scatter.4
